TPU v7x, 32 devices: a whole 2x2x4 slice. The times are simulated.
32 devices in a mesh: dp: 4 (over z), fsdp: 8 (over y, x, core).
Axes of the slice: x: 2, y: 2, z: 4, core: 2. Of those that a mesh axis runs over, the one named last changes fastest.
Arguments:
- tokens: bfloat16 [32, 1024, 768], P(('dp', 'fsdp')), may hold values from -6 to 6
- encoder_states: bfloat16 [32, 128, 768], P(('dp', 'fsdp')), may hold values from -6 to 6
- lengths: int32 [32], replicated, may hold values from 1 to 1024, as said below
- dealing: int32 [32], replicated, may hold values from 0 to 31, as said below
- cotangent: bfloat16 [32, 1024, 768], P(('dp', 'fsdp')), may hold values from -6 to 6
- w_query: bfloat16 [768, 768], P(('dp', 'fsdp')), may hold values from -0.109375 to 0.109375
- w_key: bfloat16 [768, 768], P(('dp', 'fsdp')), may hold values from -0.109375 to 0.109375
- w_value: bfloat16 [768, 768], P(('dp', 'fsdp')), may hold values from -0.21875 to 0.21875
- w_out: bfloat16 [768, 768], P(('dp', 'fsdp')), may hold values from -1 to 1
- c_query: bfloat16 [768, 768], P(('dp', 'fsdp')), may hold values from -0.109375 to 0.109375
- c_key: bfloat16 [768, 768], P(('dp', 'fsdp')), may hold values from -0.109375 to 0.109375
- c_value: bfloat16 [768, 768], P(('dp', 'fsdp')), may hold values from -0.21875 to 0.21875
- c_out: bfloat16 [768, 768], P(('dp', 'fsdp')), may hold values from -1 to 1
- w_in: bfloat16 [768, 3072], P(None, ('dp', 'fsdp')), may hold values from -0.21875 to 0.21875
- w_down: bfloat16 [3072, 768], P(('dp', 'fsdp')), may hold values from -0.15625 to 0.15625
- gain_self: bfloat16 [768], P(('dp', 'fsdp')), may hold values from 0.5 to 1.5
- gain_cross: bfloat16 [768], P(('dp', 'fsdp')), may hold values from 0.5 to 1.5
- gain_ffn: bfloat16 [768], P(('dp', 'fsdp')), may hold values from 0.5 to 1.5
- bias_table: bfloat16 [384], P(('dp', 'fsdp')), may hold values from -4 to 4
Outputs:
- output: float32 [32, 1024, 768], P(('dp', 'fsdp'))
- input_grad: float32 [32, 1024, 768], P(('dp', 'fsdp'))
- encoder_grad: float32 [32, 128, 768], P(('dp', 'fsdp'))
- grad_w_query: float32 [768, 768], P(('dp', 'fsdp'))
- grad_w_key: float32 [768, 768], P(('dp', 'fsdp'))
- grad_w_value: float32 [768, 768], P(('dp', 'fsdp'))
- grad_w_out: float32 [768, 768], P(('dp', 'fsdp'))
- grad_c_query: float32 [768, 768], P(('dp', 'fsdp'))
- grad_c_key: float32 [768, 768], P(('dp', 'fsdp'))
- grad_c_value: float32 [768, 768], P(('dp', 'fsdp'))
- grad_c_out: float32 [768, 768], P(('dp', 'fsdp'))
- grad_w_in: float32 [768, 3072], P(None, ('dp', 'fsdp'))
- grad_w_down: float32 [3072, 768], P(('dp', 'fsdp'))
- grad_gain_self: float32 [768], P(('dp', 'fsdp'))
- grad_gain_cross: float32 [768], P(('dp', 'fsdp'))
- grad_gain_ffn: float32 [768], P(('dp', 'fsdp'))
- grad_bias_table: float32 [384], P(('dp', 'fsdp'))
Inputs may be any that keep to these rules, and one draw needn't show every extreme that they name: `lengths`: the largest length equals 1024. dealing is a permutation. Slot p sits on device p of the joined axes dp+fsdp, sequence g on device g. Devices whose dp indices differ only in the lowest bit and whose fsdp index is equal form a pair; dealing either leaves the two sequences of a pair in place or exchanges them.
All inputs are finite; a program needn't handle non-finite values.
Results may differ from a plain program's by a relative error of at most 0.029.
Values may be sent and summed in bfloat16 or wider, within the bound.
A program may use at most 512 MiB of HBM per device.

v0:
```python
import math

import jax
import jax.numpy as jnp
from jax import lax
from jax.sharding import PartitionSpec as P

H = 12
DH = 64
NB = 32
MAXDIST = 128


EPSILON = 1e-06
MASKED = -1e30


def from_partner(block, axis, apart):
    count = lax.axis_size(axis)
    route = []
    for low in range(count):
        high = low | 1 << apart
        if high != low and high < count:
            route += [(low, high), (high, low)]
    return lax.ppermute(block, axis, route)


def bucket_of(distance):
    exact_count = NB // 2
    bucket = jnp.minimum(distance, exact_count)
    for level_idx in range(1, exact_count):
        threshold = int(
            math.ceil(exact_count * (MAXDIST / exact_count) ** (level_idx / exact_count))
        )
        bucket = bucket + (distance >= threshold).astype(jnp.int32)
    return bucket


def normalize(values_in, gain_vec):
    inv_rms = lax.rsqrt(jnp.mean(values_in * values_in, axis=-1, keepdims=True) + EPSILON)
    return ((values_in * inv_rms * gain_vec).astype(jnp.bfloat16), inv_rms)


def norm_back(grad_in, values_in, inv_rms, gain_vec):
    unit_rows = values_in * inv_rms
    gain_grad = jnp.sum(grad_in * unit_rows, axis=0)
    scaled_grad = grad_in * gain_vec
    return (
        inv_rms
        * (scaled_grad - unit_rows * jnp.mean(scaled_grad * unit_rows, axis=-1, keepdims=True)),
        gain_grad,
    )


def matmul(left_op, right_op):
    return jnp.dot(left_op, right_op, preferred_element_type=jnp.float32)


def matmul_tn(left_op, right_op):
    return lax.dot_general(
        left_op, right_op, (((0,), (0,)), ((), ())), preferred_element_type=jnp.float32
    )


def matmul_nt(left_op, right_op):
    return lax.dot_general(
        left_op, right_op, (((1,), (1,)), ((), ())), preferred_element_type=jnp.float32
    )


def split_heads(matrix):
    return matrix.reshape(matrix.shape[0], H, DH)


def diag_sums(grad_scores, start_row):
    head_count, row_count, key_count = grad_scores.shape
    width = MAXDIST
    padded = jnp.pad(grad_scores, ((0, 0), (0, 0), (width, 0)))
    band = padded[:, :, start_row + 1 : start_row + row_count + width]
    line = row_count + width - 1
    flat_view = jnp.pad(band.reshape(head_count, row_count * line), ((0, 0), (0, row_count)))
    sheared = flat_view.reshape(head_count, row_count, line + 1)
    return jnp.sum(sheared[:, :, :width], axis=1)[:, ::-1]


def score_block(query_block, key_rows, start_row, bias_dist, seq_length):
    raw_scores = jnp.einsum(
        "qhd,khd->hqk", query_block, key_rows, preferred_element_type=jnp.float32
    )
    if bias_dist is None:
        return raw_scores
    row_pos = start_row + jnp.arange(query_block.shape[0], dtype=jnp.int32)
    key_pos = jnp.arange(key_rows.shape[0], dtype=jnp.int32)
    distance = row_pos[:, None] - key_pos[None, :]
    allowed = (distance >= 0) & (key_pos[None, :] < seq_length)
    near_bias = jnp.take(bias_dist, jnp.maximum(distance, 0), axis=1)
    return jnp.where(allowed[None], raw_scores + near_bias, MASKED)


def attend_forward(queries, key_rows, value_rows, block, bias_dist, seq_length):
    outputs = []
    sums = []
    for start_row in range(0, queries.shape[0], block):
        end_row = start_row + block
        span = key_rows.shape[0] if bias_dist is None else end_row
        scores = score_block(
            queries[start_row:end_row], key_rows[:span], start_row, bias_dist, seq_length
        )
        row_max = jnp.max(scores, axis=-1, keepdims=True)
        weights_exp = jnp.exp(scores - row_max)
        row_total = jnp.sum(weights_exp, axis=-1, keepdims=True)
        attn_probs = (weights_exp / row_total).astype(jnp.bfloat16)
        outputs.append(
            jnp.einsum(
                "hqk,khd->qhd", attn_probs, value_rows[:span], preferred_element_type=jnp.float32
            )
        )
        sums.append(row_max + jnp.log(row_total))
    merged = jnp.concatenate(outputs, axis=0)
    return (merged.reshape(merged.shape[0], H * DH).astype(jnp.bfloat16), sums)


def attend_backward(queries, key_rows, value_rows, grad_out, block, bias_dist, seq_length, sums):
    key_count = key_rows.shape[0]
    grad_keys = jnp.zeros(key_rows.shape, jnp.float32)
    grad_values = jnp.zeros(value_rows.shape, jnp.float32)
    dist_grad = jnp.zeros((H, MAXDIST), jnp.float32)
    query_gradient_rows = []
    for block_idx, start_row in enumerate(range(0, queries.shape[0], block)):
        end_row = start_row + block
        span = key_count if bias_dist is None else end_row
        query_block = queries[start_row:end_row]
        scores = score_block(query_block, key_rows[:span], start_row, bias_dist, seq_length)
        attn_probs = jnp.exp(scores - sums[block_idx])
        low_probs = attn_probs.astype(jnp.bfloat16)
        grad_block = split_heads(grad_out[start_row:end_row])
        grad_values = grad_values.at[:span].add(
            jnp.einsum("hqk,qhd->khd", low_probs, grad_block, preferred_element_type=jnp.float32)
        )
        grad_probs = jnp.einsum(
            "qhd,khd->hqk", grad_block, value_rows[:span], preferred_element_type=jnp.float32
        )
        grad_scores = attn_probs * (
            grad_probs - jnp.sum(attn_probs * grad_probs, axis=-1, keepdims=True)
        )
        if bias_dist is not None:
            dist_grad = dist_grad + diag_sums(grad_scores, start_row)
        low_scores = grad_scores.astype(jnp.bfloat16)
        query_gradient_rows.append(
            jnp.einsum(
                "hqk,khd->qhd", low_scores, key_rows[:span], preferred_element_type=jnp.float32
            )
        )
        grad_keys = grad_keys.at[:span].add(
            jnp.einsum("hqk,qhd->khd", low_scores, query_block, preferred_element_type=jnp.float32)
        )
    merged = jnp.concatenate(query_gradient_rows, axis=0)
    return (
        merged.reshape(merged.shape[0], H * DH).astype(jnp.bfloat16),
        grad_keys.reshape(key_count, H * DH).astype(jnp.bfloat16),
        grad_values.reshape(key_count, H * DH).astype(jnp.bfloat16),
        dist_grad,
    )


def body(
    tokens,
    encoder_states,
    lengths,
    dealing,
    cotangent,
    w_query,
    w_key,
    w_value,
    w_out,
    c_query,
    c_key,
    c_value,
    c_out,
    w_in,
    w_down,
    gain_self,
    gain_cross,
    gain_ffn,
    bias_table,
):
    fsdp_size = lax.axis_size("fsdp")
    dp_index = lax.axis_index("dp")
    fsdp_index = lax.axis_index("fsdp")
    seq_count, seq_len, model = tokens.shape
    enc_len = encoder_states.shape[1]
    block = min(512, seq_len)
    own_dev = dp_index * fsdp_size + fsdp_index
    partner_dp = dp_index + 1 - 2 * (dp_index % 2)
    partner_dev = partner_dp * fsdp_size + fsdp_index
    slot_range = jnp.arange(seq_count, dtype=jnp.int32)
    own_ids = own_dev * seq_count + slot_range
    sources = lax.dynamic_slice_in_dim(dealing, own_dev * seq_count, seq_count)
    partner_sources = lax.dynamic_slice_in_dim(dealing, partner_dev * seq_count, seq_count)
    outgoing_selection = (partner_sources[:, None] == own_ids[None, :]).astype(jnp.bfloat16)
    local_selection = (sources[:, None] == own_ids[None, :]).astype(jnp.bfloat16)
    is_remote = 1.0 - jnp.sum(local_selection.astype(jnp.float32), axis=1)
    send_tokens = jnp.einsum(
        "ep,pxo->exo", outgoing_selection, tokens, preferred_element_type=jnp.float32
    ).astype(jnp.bfloat16)
    send_grads = jnp.einsum(
        "ep,pxo->exo", outgoing_selection, cotangent, preferred_element_type=jnp.float32
    ).astype(jnp.bfloat16)
    got_tokens, got_grads = from_partner((send_tokens, send_grads), "dp", 0)
    token_rows = jnp.einsum(
        "ep,pxo->exo", local_selection, tokens, preferred_element_type=jnp.float32
    ) + is_remote[:, None, None] * got_tokens.astype(jnp.float32)
    grad_rows = jnp.einsum(
        "ep,pxo->exo", local_selection, cotangent, preferred_element_type=jnp.float32
    ) + is_remote[:, None, None] * got_grads.astype(jnp.float32)
    seq_lengths = jnp.take(lengths, sources)
    positions = jnp.arange(seq_len, dtype=jnp.int32)
    rows_total = seq_count * seq_len
    row_valid = (
        (positions[None, :] < seq_lengths[:, None]).astype(jnp.float32).reshape(rows_total, 1)
    )
    (
        query_weight,
        key_weight,
        value_weight,
        out_weight,
        cross_query,
        cross_key,
        cross_value,
        cross_out,
        in_weight,
        down_weight,
        self_gain,
        cross_gain,
        ffn_gain,
        table_flat,
    ) = (
        lax.all_gather(w_query, ("dp", "fsdp"), axis=0, tiled=True),
        lax.all_gather(w_key, ("dp", "fsdp"), axis=0, tiled=True),
        lax.all_gather(w_value, ("dp", "fsdp"), axis=0, tiled=True),
        lax.all_gather(w_out, ("dp", "fsdp"), axis=0, tiled=True),
        lax.all_gather(c_query, ("dp", "fsdp"), axis=0, tiled=True),
        lax.all_gather(c_key, ("dp", "fsdp"), axis=0, tiled=True),
        lax.all_gather(c_value, ("dp", "fsdp"), axis=0, tiled=True),
        lax.all_gather(c_out, ("dp", "fsdp"), axis=0, tiled=True),
        lax.all_gather(w_in, ("dp", "fsdp"), axis=1, tiled=True),
        lax.all_gather(w_down, ("dp", "fsdp"), axis=0, tiled=True),
        lax.all_gather(gain_self, ("dp", "fsdp"), axis=0, tiled=True),
        lax.all_gather(gain_cross, ("dp", "fsdp"), axis=0, tiled=True),
        lax.all_gather(gain_ffn, ("dp", "fsdp"), axis=0, tiled=True),
        lax.all_gather(bias_table, ("dp", "fsdp"), axis=0, tiled=True),
    )
    table_full = table_flat.astype(jnp.float32).reshape(NB, H)
    bucket_hot = (bucket_of(positions)[:, None] == jnp.arange(NB, dtype=jnp.int32)[None, :]).astype(
        jnp.float32
    )
    bias_dist = jnp.dot(bucket_hot, table_full, precision=lax.Precision.HIGHEST).T
    base_rows = token_rows.reshape(rows_total, model)
    normed_one, inv_one = normalize(base_rows, self_gain.astype(jnp.float32))
    queries = matmul(normed_one, query_weight).astype(jnp.bfloat16)
    key_rows = matmul(normed_one, key_weight).astype(jnp.bfloat16)
    value_rows = matmul(normed_one, value_weight).astype(jnp.bfloat16)
    slot_idx = 0
    piece, sums = attend_forward(
        split_heads(queries),
        split_heads(key_rows),
        split_heads(value_rows),
        block,
        bias_dist,
        seq_lengths[slot_idx],
    )
    attended_parts = piece
    self_sums = [sums]
    after_self = base_rows + matmul(attended_parts, out_weight)
    normed_two, inv_two = normalize(after_self, cross_gain.astype(jnp.float32))
    cross_queries = matmul(normed_two, cross_query).astype(jnp.bfloat16)
    enc_rows = encoder_states.reshape(seq_count * enc_len, model)
    cross_keys = matmul(enc_rows, cross_key).astype(jnp.bfloat16)
    cross_values = matmul(enc_rows, cross_value).astype(jnp.bfloat16)
    piece, sums = attend_forward(
        split_heads(cross_queries),
        split_heads(cross_keys),
        split_heads(cross_values),
        block,
        None,
        None,
    )
    cross_sums = [sums]
    after_cross = after_self + matmul(piece, cross_out)
    normed_three, inv_three = normalize(after_cross, ffn_gain.astype(jnp.float32))
    pre_ffn = matmul(normed_three, in_weight)
    hidden = jax.nn.gelu(pre_ffn).astype(jnp.bfloat16)
    result_rows = (after_cross + matmul(hidden, down_weight)) * row_valid
    (
        query_weight,
        key_weight,
        value_weight,
        out_weight,
        cross_query,
        cross_key,
        cross_value,
        cross_out,
        in_weight,
        down_weight,
        self_gain,
        cross_gain,
        ffn_gain,
        table_flat,
    ) = (
        lax.all_gather(w_query, ("dp", "fsdp"), axis=0, tiled=True),
        lax.all_gather(w_key, ("dp", "fsdp"), axis=0, tiled=True),
        lax.all_gather(w_value, ("dp", "fsdp"), axis=0, tiled=True),
        lax.all_gather(w_out, ("dp", "fsdp"), axis=0, tiled=True),
        lax.all_gather(c_query, ("dp", "fsdp"), axis=0, tiled=True),
        lax.all_gather(c_key, ("dp", "fsdp"), axis=0, tiled=True),
        lax.all_gather(c_value, ("dp", "fsdp"), axis=0, tiled=True),
        lax.all_gather(c_out, ("dp", "fsdp"), axis=0, tiled=True),
        lax.all_gather(w_in, ("dp", "fsdp"), axis=1, tiled=True),
        lax.all_gather(w_down, ("dp", "fsdp"), axis=0, tiled=True),
        lax.all_gather(gain_self, ("dp", "fsdp"), axis=0, tiled=True),
        lax.all_gather(gain_cross, ("dp", "fsdp"), axis=0, tiled=True),
        lax.all_gather(gain_ffn, ("dp", "fsdp"), axis=0, tiled=True),
        lax.all_gather(bias_table, ("dp", "fsdp"), axis=0, tiled=True),
    )
    grad_res = grad_rows.reshape(rows_total, model) * row_valid
    grad_low = grad_res.astype(jnp.bfloat16)
    grad_down = matmul_tn(hidden, grad_low)
    grad_hidden = matmul_nt(grad_low, down_weight)
    unused_value, gelu_pull = jax.vjp(jax.nn.gelu, pre_ffn)
    grad_pre = gelu_pull(grad_hidden)[0].astype(jnp.bfloat16)
    grad_in = matmul_tn(normed_three, grad_pre)
    part_three, grad_ffn_gain = norm_back(
        matmul_nt(grad_pre, in_weight), after_cross, inv_three, ffn_gain.astype(jnp.float32)
    )
    grad_two = grad_res + part_three
    cross_low = grad_two.astype(jnp.bfloat16)
    grad_cross_out = matmul_tn(piece, cross_low)
    grad_mixed = matmul_nt(cross_low, cross_out).astype(jnp.bfloat16)
    slot_idx = 0
    grad_q, grad_k, grad_v, unused_dist = attend_backward(
        split_heads(cross_queries),
        split_heads(cross_keys),
        split_heads(cross_values),
        grad_mixed,
        block,
        None,
        None,
        cross_sums[slot_idx],
    )
    cq_parts = grad_q
    ck_parts = grad_k
    cv_parts = grad_v
    grad_cross_query = matmul_tn(normed_two, cq_parts)
    grad_cross_key = matmul_tn(enc_rows, ck_parts)
    grad_cross_value = matmul_tn(enc_rows, cv_parts)
    encoder_grad = (matmul_nt(ck_parts, cross_key) + matmul_nt(cv_parts, cross_value)).reshape(
        seq_count, enc_len, model
    )
    part_two, grad_cross_gain = norm_back(
        matmul_nt(cq_parts, cross_query), after_self, inv_two, cross_gain.astype(jnp.float32)
    )
    grad_one = grad_two + part_two
    self_low = grad_one.astype(jnp.bfloat16)
    grad_self_out = matmul_tn(attended_parts, self_low)
    grad_attended = matmul_nt(self_low, out_weight).astype(jnp.bfloat16)
    slot_idx = 0
    grad_q, grad_k, grad_v, dist_grad = attend_backward(
        split_heads(queries),
        split_heads(key_rows),
        split_heads(value_rows),
        grad_attended,
        block,
        bias_dist,
        seq_lengths[slot_idx],
        self_sums[slot_idx],
    )
    grad_query_w = matmul_tn(normed_one, grad_q)
    grad_key_w = matmul_tn(normed_one, grad_k)
    grad_value_w = matmul_tn(normed_one, grad_v)
    back_one = (
        matmul_nt(grad_q, query_weight)
        + matmul_nt(grad_k, key_weight)
        + matmul_nt(grad_v, value_weight)
    )
    part_one, grad_self_gain = norm_back(
        back_one, base_rows, inv_one, self_gain.astype(jnp.float32)
    )
    input_rows = grad_one + part_one
    near_part = dist_grad[:, : MAXDIST - 1]
    far_part = -jnp.sum(near_part, axis=1, keepdims=True)
    band_column = jnp.concatenate([near_part, far_part], axis=1)
    band_hot = (
        bucket_of(jnp.arange(MAXDIST, dtype=jnp.int32))[:, None]
        == jnp.arange(NB, dtype=jnp.int32)[None, :]
    ).astype(jnp.float32)
    grad_table = jnp.dot(band_hot.T, band_column.T, precision=lax.Precision.HIGHEST).reshape(NB * H)
    (
        sum_query,
        sum_key,
        sum_value,
        sum_out,
        sum_cquery,
        sum_ckey,
        sum_cvalue,
        sum_cout,
        sum_in,
        sum_down,
        sum_gself,
        sum_gcross,
        sum_gffn,
        sum_table,
    ) = (
        lax.psum_scatter(grad_query_w, ("dp", "fsdp"), scatter_dimension=0, tiled=True),
        lax.psum_scatter(grad_key_w, ("dp", "fsdp"), scatter_dimension=0, tiled=True),
        lax.psum_scatter(grad_value_w, ("dp", "fsdp"), scatter_dimension=0, tiled=True),
        lax.psum_scatter(grad_self_out, ("dp", "fsdp"), scatter_dimension=0, tiled=True),
        lax.psum_scatter(grad_cross_query, ("dp", "fsdp"), scatter_dimension=0, tiled=True),
        lax.psum_scatter(grad_cross_key, ("dp", "fsdp"), scatter_dimension=0, tiled=True),
        lax.psum_scatter(grad_cross_value, ("dp", "fsdp"), scatter_dimension=0, tiled=True),
        lax.psum_scatter(grad_cross_out, ("dp", "fsdp"), scatter_dimension=0, tiled=True),
        lax.psum_scatter(grad_in, ("dp", "fsdp"), scatter_dimension=1, tiled=True),
        lax.psum_scatter(grad_down, ("dp", "fsdp"), scatter_dimension=0, tiled=True),
        lax.psum_scatter(grad_self_gain, ("dp", "fsdp"), scatter_dimension=0, tiled=True),
        lax.psum_scatter(grad_cross_gain, ("dp", "fsdp"), scatter_dimension=0, tiled=True),
        lax.psum_scatter(grad_ffn_gain, ("dp", "fsdp"), scatter_dimension=0, tiled=True),
        lax.psum_scatter(grad_table, ("dp", "fsdp"), scatter_dimension=0, tiled=True),
    )
    result_slot_table = result_rows.reshape(seq_count, seq_len, model)
    input_slot_table = input_rows.reshape(seq_count, seq_len, model)
    remote_mask = is_remote[:, None, None]
    backward_output_rows, backward_input_rows = (
        from_partner((result_slot_table * remote_mask).astype(jnp.bfloat16), "dp", 0).astype(
            jnp.float32
        ),
        from_partner((input_slot_table * remote_mask).astype(jnp.bfloat16), "dp", 0).astype(
            jnp.float32
        ),
    )
    local_wide = local_selection.astype(jnp.float32)
    outgoing_wide = outgoing_selection.astype(jnp.float32)
    output = jnp.einsum(
        "pj,pyu->jyu", local_wide, result_slot_table, precision=lax.Precision.HIGHEST
    ) + jnp.einsum(
        "pj,pyu->jyu", outgoing_wide, backward_output_rows, precision=lax.Precision.HIGHEST
    )
    input_grad = jnp.einsum(
        "pj,pyu->jyu", local_wide, input_slot_table, precision=lax.Precision.HIGHEST
    ) + jnp.einsum(
        "pj,pyu->jyu", outgoing_wide, backward_input_rows, precision=lax.Precision.HIGHEST
    )
    return (
        output,
        input_grad,
        encoder_grad,
        sum_query,
        sum_key,
        sum_value,
        sum_out,
        sum_cquery,
        sum_ckey,
        sum_cvalue,
        sum_cout,
        sum_in,
        sum_down,
        sum_gself,
        sum_gcross,
        sum_gffn,
        sum_table,
    )


def solution(mesh):
    in_specs = (
        P(("dp", "fsdp"), None, None),
        P(("dp", "fsdp"), None, None),
        P(),
        P(),
        P(("dp", "fsdp"), None, None),
        P(("dp", "fsdp"), None),
        P(("dp", "fsdp"), None),
        P(("dp", "fsdp"), None),
        P(("dp", "fsdp"), None),
        P(("dp", "fsdp"), None),
        P(("dp", "fsdp"), None),
        P(("dp", "fsdp"), None),
        P(("dp", "fsdp"), None),
        P(None, ("dp", "fsdp")),
        P(("dp", "fsdp"), None),
        P(("dp", "fsdp")),
        P(("dp", "fsdp")),
        P(("dp", "fsdp")),
        P(("dp", "fsdp")),
    )
    out_specs = (
        P(("dp", "fsdp"), None, None),
        P(("dp", "fsdp"), None, None),
        P(("dp", "fsdp"), None, None),
        P(("dp", "fsdp"), None),
        P(("dp", "fsdp"), None),
        P(("dp", "fsdp"), None),
        P(("dp", "fsdp"), None),
        P(("dp", "fsdp"), None),
        P(("dp", "fsdp"), None),
        P(("dp", "fsdp"), None),
        P(("dp", "fsdp"), None),
        P(None, ("dp", "fsdp")),
        P(("dp", "fsdp"), None),
        P(("dp", "fsdp")),
        P(("dp", "fsdp")),
        P(("dp", "fsdp")),
        P(("dp", "fsdp")),
    )
    return jax.shard_map(body, mesh=mesh, in_specs=in_specs, out_specs=out_specs, check_vma=False)
```

profile of v0, /device:TPU:0, one launch (start us, length us, event | category | flops | bytes accessed | tf_op | source)
XLA Modules:
  0.0 4301.3 jit_solution(303111141155348)
XLA Ops:
  29.3 89.0 %all-reduce.14 = (bf16[768]{0:T(1024)(128)(2,1)S(1)}, bf16[384]{0:T(512)(128)(2,1)S(1)}, bf16[768]{0:T(1024)(128)(2,1)}, bf16[768]{0:T(1024)(128)(2,1)}) all-reduce(bf16[768]{0:T(1024)(128)(2,1)S(1)} %dynamic-update-slice.19, bf16[384]{0:T(512)(128)(2,1)S(1)} %dynamic-update-slice.20, ...), channel_id=1, replica_groups=mesh['dp'=4,'fsdp'=8] {'dp','fsdp'}, use_global_device_ids=true, to_apply=%add.5 | all-reduce | flops 2688 | bytes 10752
  119.4 1719.4 %gather_fusion.1 = f32[524288,12]{1,0:T(8,128)} fusion(f32[12,1024]{0,1:T(8,128)S(1)} %fusion.110, s32[524288]{0:T(1024)S(1)} %broadcast_clamp_fusion), kind=kCustom, calls=%fused_computation.1.clone | custom fusion | bytes 52428800 | tf_op jit(solution)/shard_map/jit(_take)/gather | solution.py:96
  1838.8 144.2 %copy.210 = f32[512,1024,12]{1,0,2:T(8,128)} copy(f32[512,1024,12]{2,1,0:T(8,128)} %bitcast.18) | data formatting | bytes 50331648 | tf_op jit(solution)/shard_map/jit(_take)/gather | solution.py:96
  1984.9 860.0 %gather_fusion = f32[262144,12]{1,0:T(8,128)} fusion(f32[12,1024]{0,1:T(8,128)S(1)} %fusion.110, s32[262144]{0:T(1024)S(1)} %copy-done.41), kind=kCustom, calls=%fused_computation.clone | custom fusion | bytes 26214400 | tf_op jit(solution)/shard_map/jit(_take)/gather | solution.py:96
  2845.0 73.5 %copy.155 = f32[512,512,12]{0,1,2:T(8,128)} copy(f32[512,512,12]{2,1,0:T(8,128)} %bitcast.12) | data formatting | bytes 25165824 | tf_op jit(solution)/shard_map/jit(_take)/gather | solution.py:96
  2947.8 17.6 fusion.183
  2965.3 11.0 fusion.1
  2976.4 11.5 fusion.89
  3035.1 11.0 fusion.176
  3046.1 18.6 fusion.9
  3095.1 18.1 multiply_reduce_fusion
  3113.3 26.0 subtract_multiply_fusion
  3139.3 13.1 fusion.80
  3187.5 11.0 fusion.33
  3209.4 11.1 fusion.32
  3266.9 14.3 fusion.117
  3281.7 15.0 slice.268
  3296.7 11.2 add_multiply_fusion
  3324.8 25.2 reshape.840
  3367.2 12.1 slice.273
  3379.3 13.4 pad_slice_fusion
  3392.7 15.8 copy.181
  3408.5 25.4 reshape.838
  3450.8 12.0 slice.272
  3471.5 40.4 all-reduce.13
  3531.3 63.1 %reduce-scatter.21.cloned.1.call-done = f32[24,768]{1,0:T(8,128)} async-done(((f32[768,768]{1,0:T(8,128)}), f32[24,768]{1,0:T(8,128)}) %reduce-scatter.21.cloned.1.call-update) | async-done | bytes 73744 | tf_op jit(solution)/shard_map/reduce_scatter | solution.py:416
  3594.4 103.8 %reduce-scatter.23.cloned.1.call-done = f32[24,768]{1,0:T(8,128)} async-done(((f32[768,768]{1,0:T(8,128)}), f32[24,768]{1,0:T(8,128)}) %reduce-scatter.23.cloned.1.call-update) | async-done | bytes 73744 | tf_op jit(solution)/shard_map/reduce_scatter | solution.py:417
  3698.1 104.7 %reduce-scatter.31.cloned.1.call-done = f32[24,768]{1,0:T(8,128)} async-done(((f32[768,768]{1,0:T(8,128)}), f32[24,768]{1,0:T(8,128)}) %reduce-scatter.31.cloned.1.call-update) | async-done | bytes 73744
  3802.8 103.7 %reduce-scatter.33.cloned.1.call-done = f32[24,768]{1,0:T(8,128)} async-done(((f32[768,768]{1,0:T(8,128)}), f32[24,768]{1,0:T(8,128)}) %reduce-scatter.33.cloned.1.call-update) | async-done | bytes 73744
  3906.5 104.7 %reduce-scatter.25.cloned.1.call-done = f32[24,768]{1,0:T(8,128)} async-done(((f32[768,768]{1,0:T(8,128)}), f32[24,768]{1,0:T(8,128)}) %reduce-scatter.25.cloned.1.call-update) | async-done | bytes 73744 | tf_op jit(solution)/shard_map/reduce_scatter | solution.py:420
  4011.2 141.0 %reduce-scatter.27.cloned.1.call-done = f32[768,96]{0,1:T(8,128)} async-done(((f32[768,3072]{0,1:T(8,128)}), f32[768,96]{0,1:T(8,128)}) %reduce-scatter.27.cloned.1.call-update) | async-done | bytes 294928 | tf_op jit(solution)/shard_map/reduce_scatter | solution.py:421
  4152.2 142.1 %reduce-scatter.29.cloned.1.call-done = f32[96,768]{1,0:T(8,128)} async-done(((f32[3072,768]{1,0:T(8,128)}), f32[96,768]{1,0:T(8,128)}) %reduce-scatter.29.cloned.1.call-update) | async-done | bytes 294928 | tf_op jit(solution)/shard_map/reduce_scatter | solution.py:422
  (434 shorter events, 298.4 us)
Async XLA Ops:
  7.2 2938.2 %copy-start = (bf16[1,128,768]{2,1,0:T(8,128)(2,1)S(1)}, bf16[1,128,768]{2,1,0:T(8,128)(2,1)}, u32[]{:S(2)}) copy-start(bf16[1,128,768]{2,1,0:T(8,128)(2,1)} %param.52) | copy-start | bytes 589828
  7.2 2925.0 %all-gather.13.cloned.1.call-start = ((), (), s32[]{:S(2)}) async-start(), calls=%async_computation.11 | async-start | bytes 1216512 | tf_op jit(solution)/shard_map/all_gather | solution.py:238
  7.9 2928.3 %all-gather.11.cloned.1.call-start = ((), (), s32[]{:S(2)}) async-start(), calls=%async_computation.10 | async-start | bytes 1216512 | tf_op jit(solution)/shard_map/all_gather | solution.py:240
  8.7 2932.4 %all-gather.15.cloned.1.call-start = ((), (), s32[]{:S(2)}) async-start(), calls=%async_computation.12 | async-start | bytes 1216512 | tf_op jit(solution)/shard_map/all_gather | solution.py:239
  9.4 2935.9 %all-gather.19.cloned.1.call-start = ((), (), s32[]{:S(2)}) async-start(), calls=%async_computation.14 | async-start | bytes 1216512 | tf_op jit(solution)/shard_map/all_gather | solution.py:244
  10.0 2991.2 %all-gather.23.cloned.1.call-start = ((), (), s32[]{:S(2)}) async-start(), calls=%async_computation.16 | async-start | bytes 1216512 | tf_op jit(solution)/shard_map/all_gather | solution.py:243
  10.6 2999.5 %all-gather.17.cloned.1.call-start = ((), (), s32[]{:S(2)}) async-start(), calls=%async_computation.13 | async-start | bytes 1216512 | tf_op jit(solution)/shard_map/all_gather | solution.py:241
  11.2 3004.9 %all-gather.21.cloned.1.call-start = ((), (), s32[]{:S(2)}) async-start(), calls=%async_computation.15 | async-start | bytes 1216512 | tf_op jit(solution)/shard_map/all_gather | solution.py:242
  11.9 3014.4 %all-gather.25.cloned.1.call-start = ((), (), s32[]{:S(2)}) async-start(), calls=%async_computation.17 | async-start | bytes 1216512 | tf_op jit(solution)/shard_map/all_gather | solution.py:245
  12.7 3022.4 %all-gather.27.cloned.1.call-start = ((), (), s32[]{:S(2)}) async-start(), calls=%async_computation.18 | async-start | bytes 4866048 | tf_op jit(solution)/shard_map/all_gather | solution.py:246
  13.4 3032.6 %all-gather.29.cloned.1.call-start = ((), (), s32[]{:S(2)}) async-start(), calls=%async_computation.19 | async-start | bytes 4866048 | tf_op jit(solution)/shard_map/all_gather | solution.py:247
  18.1 2905.8 %collective-permute-start = (bf16[1,1024,768]{1,2,0:T(8,128)(2,1)}, bf16[1,1024,768]{1,2,0:T(8,128)(2,1)}, u32[]{:S(2)}, u32[]{:S(2)}) collective-permute-start(bf16[1,1024,768]{1,2,0:T(8,128)(2,1)} %fusion.26), channel_id=1, source_target_pairs={{0,8},{8,0},{16,24},{24,16},{1,9},{9,1},{17,25},{25,17},{2,10},{10... | collective-permute-start | bytes 4718600 | tf_op jit(solution)/shard_map/ppermute | solution.py:25
  24.5 3021.5 %collective-permute-start.2 = (bf16[1,1024,768]{1,2,0:T(8,128)(2,1)}, bf16[1,1024,768]{1,2,0:T(8,128)(2,1)}, u32[]{:S(2)}, u32[]{:S(2)}) collective-permute-start(bf16[1,1024,768]{1,2,0:T(8,128)(2,1)} %fusion.30), channel_id=1, source_target_pairs={{0,8},{8,0},{16,24},{24,16},{1,9},{9,1},{17,25},{25,17},{2,10},{10... | collective-permute-start | bytes 4718600 | tf_op jit(solution)/shard_map/ppermute | solution.py:25
  24.6 3506.7 %reduce-scatter.15.cloned.1.call-start = ((), (), s32[]{:S(2)}) async-start(), calls=%async_computation.20 | async-start | bytes 2433024 | tf_op jit(solution)/shard_map/reduce_scatter | solution.py:413
  1838.8 146.2 %copy-start.41 = (s32[262144]{0:T(1024)S(1)}, s32[262144]{0:T(1024)}, u32[]{:S(2)}) copy-start(s32[262144]{0:T(1024)} %broadcast_clamp_fusion.1) | copy-start | bytes 3145732
  2845.0 74.6 %copy-start.113 = (s32[32]{0:T(128)S(1)}, s32[32]{0:T(128)}, u32[]{:S(2)}) copy-start(s32[32]{0:T(128)} %param.53) | copy-start | bytes 388
  2845.0 77.0 %copy-start.102 = (bf16[768]{0:T(1024)(128)(2,1)S(1)}, bf16[768]{0:T(1024)(128)(2,1)}, u32[]{:S(2)}) copy-start(bf16[768]{0:T(1024)(128)(2,1)} %get-tuple-element.254) | copy-start | bytes 4612
  2845.0 77.0 %copy-start.101 = (bf16[768]{0:T(1024)(128)(2,1)S(1)}, bf16[768]{0:T(1024)(128)(2,1)}, u32[]{:S(2)}) copy-start(bf16[768]{0:T(1024)(128)(2,1)} %get-tuple-element.255) | copy-start | bytes 4612
  2845.0 77.1 %copy-start.96 = (s32[512]{0:T(512)S(1)}, s32[512]{0:T(512)}, u32[]{:S(2)}) copy-start(s32[512]{0:T(512)} %copy-done.95) | copy-start | bytes 6148
  2922.0 152.8 %copy-start.97 = (f32[1024]{0:T(1024)}, f32[1024]{0:T(1024)S(1)}, u32[]{:S(2)}) copy-start(f32[1024]{0:T(1024)S(1)} %fusion.171) | copy-start | bytes 12292
  3022.7 62.0 %copy-start.3 = (f32[12,512,128]{1,2,0:T(8,128)}, f32[12,512,128]{1,2,0:T(8,128)S(1)}, u32[]{:S(2)}) copy-start(f32[12,512,128]{1,2,0:T(8,128)S(1)} %get-tuple-element.281) | copy-start | bytes 9437188
  3180.6 350.7 %reduce-scatter.17.cloned.1.call-start = ((), (), s32[]{:S(2)}) async-start(), calls=%async_computation.21 | async-start | bytes 2433024 | tf_op jit(solution)/shard_map/reduce_scatter | solution.py:414
  3202.5 328.8 %reduce-scatter.19.cloned.1.call-start = ((), (), s32[]{:S(2)}) async-start(), calls=%async_computation.22 | async-start | bytes 2433024 | tf_op jit(solution)/shard_map/reduce_scatter | solution.py:415
  3224.5 369.8 %reduce-scatter.21.cloned.1.call-start = ((), (), s32[]{:S(2)}) async-start(), calls=%async_computation.23 | async-start | bytes 2433024 | tf_op jit(solution)/shard_map/reduce_scatter | solution.py:416
  3228.9 469.3 %reduce-scatter.23.cloned.1.call-start = ((), (), s32[]{:S(2)}) async-start(), calls=%async_computation.24 | async-start | bytes 2433024 | tf_op jit(solution)/shard_map/reduce_scatter | solution.py:417
  3234.3 568.5 %reduce-scatter.31.cloned.1.call-start = ((), (), s32[]{:S(2)}) async-start(), calls=%async_computation.28 | async-start | bytes 2433024
  3240.5 666.0 %reduce-scatter.33.cloned.1.call-start = ((), (), s32[]{:S(2)}) async-start(), calls=%async_computation.29 | async-start | bytes 2433024
  3250.3 760.9 %reduce-scatter.25.cloned.1.call-start = ((), (), s32[]{:S(2)}) async-start(), calls=%async_computation.25 | async-start | bytes 2433024 | tf_op jit(solution)/shard_map/reduce_scatter | solution.py:420
  3254.6 897.5 %reduce-scatter.27.cloned.1.call-start = ((), (), s32[]{:S(2)}) async-start(), calls=%async_computation.26 | async-start | bytes 9732096 | tf_op jit(solution)/shard_map/reduce_scatter | solution.py:421
  3265.5 1028.8 %reduce-scatter.29.cloned.1.call-start = ((), (), s32[]{:S(2)}) async-start(), calls=%async_computation.27 | async-start | bytes 9732096 | tf_op jit(solution)/shard_map/reduce_scatter | solution.py:422
  3309.6 209.2 %collective-permute-start.1 = (bf16[1,1024,768]{1,2,0:T(8,128)(2,1)}, bf16[1,1024,768]{1,2,0:T(8,128)(2,1)}, u32[]{:S(2)}, u32[]{:S(2)}) collective-permute-start(bf16[1,1024,768]{1,2,0:T(8,128)(2,1)} %fusion.58), channel_id=1, source_target_pairs={{0,8},{8,0},{16,24},{24,16},{1,9},{9,1},{17,25},{25,17},{2,10},{10... | collective-permute-start | bytes 4718600 | tf_op jit(solution)/shard_map/ppermute | solution.py:25
  3323.8 202.1 %collective-permute-start.3 = (bf16[1,1024,768]{1,2,0:T(8,128)(2,1)}, bf16[1,1024,768]{1,2,0:T(8,128)(2,1)}, u32[]{:S(2)}, u32[]{:S(2)}) collective-permute-start(bf16[1,1024,768]{1,2,0:T(8,128)(2,1)} %get-tuple-element.258), channel_id=1, source_target_pairs={{0,8},{8,0},{16,24},{24,16},{1,9},{9,1},{17,25},{25,17},{2,10},{10... | collective-permute-start | bytes 4718600 | tf_op jit(solution)/shard_map/ppermute | solution.py:25
  (109 other events, 685.4 us)
Sparse Core Ops, SparseCore 0:
  10.9 57.9 all-gather.12
  71.8 53.3 all-gather.10
  128.1 53.1 all-gather.14
  184.0 52.9 all-gather.18
  239.8 52.9 all-gather.22
  295.6 52.9 all-gather.16
  351.4 52.9 all-gather.20
  407.3 52.9 all-gather.24
  463.3 62.5 all-gather.26
  528.6 62.4 all-gather.28
  3180.7 98.3 reduce-scatter.14
  3285.7 100.0 reduce-scatter.16
  3391.6 98.0 reduce-scatter.18
  3496.3 98.0 reduce-scatter.20
  3600.1 97.9 reduce-scatter.22
  3704.7 98.0 reduce-scatter.30
  3808.5 97.9 reduce-scatter.32
  3913.0 98.1 reduce-scatter.24
  4017.7 134.4 reduce-scatter.26
  4159.5 134.7 reduce-scatter.28
where the time goes:
time: 4310 us; the launch traced here: 4300 us
  local copies, waits for them, and re-layouts  3010 us (70%)
  waiting for transfers between devices  769 us (18%)
  matrix products  279 us (6%)
  blocking collectives  129 us (3%)
  other arithmetic  91.7 us (2%)
    gather x4, local copies, waits for them, and re-layouts, score_block(): near_bias = jnp.take(bias_dist, jnp.maximum(distance, 0), axis=1)  2800 us
    unnamed x22, waiting for transfers between devices  214 us
    reduce_scatter x1, waiting for transfers between devices, body(): lax.psum_scatter(grad_down, ('dp', 'fsdp'), scatter_dimension=0, tiled=True)  142 us
    reduce_scatter x1, waiting for transfers between devices, body(): lax.psum_scatter(grad_in, ('dp', 'fsdp'), scatter_dimension=1, tiled=True)  141 us
    unnamed x2, blocking collectives  129 us
    reduce_scatter x1, waiting for transfers between devices, body(): lax.psum_scatter(grad_cross_out, ('dp', 'fsdp'), scatter_dimension=0, til...  105 us
    reduce_scatter x1, waiting for transfers between devices, body(): lax.psum_scatter(grad_cross_query, ('dp', 'fsdp'), scatter_dimension=0, t...  104 us
  transfers between devices with their start and end apart: 24, of which 7 were waited for; matrix products, arithmetic and copies ran while one was open for 75% of the time, Pallas kernels for 0%

commit v1 on v0

v1 whole, which is shorter than its diff:
```python
import functools
import math

import jax
import jax.numpy as jnp
from jax import lax
from jax.experimental import pallas as pl
from jax.experimental.pallas import tpu as pltpu
from jax.sharding import PartitionSpec as P

H = 12
DH = 64
NB = 32
MAXDIST = 128
EPSILON = 1e-06
MASKED = -1e30
LANES = 128
ROWS = 256
F32 = jnp.float32
BF16 = jnp.bfloat16
GELU_C = math.sqrt(2.0 / math.pi)
GELU_A = 0.044715


def bucket_of(distance):
    exact_count = NB // 2
    bucket = jnp.minimum(distance, exact_count)
    for level_idx in range(1, exact_count):
        threshold = int(
            math.ceil(exact_count * (MAXDIST / exact_count) ** (level_idx / exact_count))
        )
        bucket = bucket + (distance >= threshold).astype(jnp.int32)
    return bucket


def nn(left_op, right_op):
    return lax.dot_general(
        left_op, right_op, (((1,), (0,)), ((), ())), preferred_element_type=F32
    )


def nt(left_op, right_op):
    return lax.dot_general(
        left_op, right_op, (((1,), (1,)), ((), ())), preferred_element_type=F32
    )


def tn(left_op, right_op):
    return lax.dot_general(
        left_op, right_op, (((0,), (0,)), ((), ())), preferred_element_type=F32
    )


def unit_rows(values_in):
    inv_rms = lax.rsqrt(jnp.mean(values_in * values_in, axis=-1, keepdims=True) + EPSILON)
    return values_in * inv_rms, inv_rms


def norm_back(grad_in, unit, inv_rms, gain_vec):
    scaled = grad_in * gain_vec
    through = inv_rms * (scaled - unit * jnp.mean(scaled * unit, axis=-1, keepdims=True))
    return through, jnp.sum(grad_in * unit, axis=0, keepdims=True)


def head_lane(shape, which):
    lane = lax.broadcasted_iota(jnp.int32, shape, len(shape) - 1)
    return (lane // DH) == which


def self_forward_kernel(
    length_ref, x_ref, gain_ref, wq_ref, wk_ref, wv_ref, far_ref, near_ref,
    q_ref, k_ref, v_ref, o_ref, p_ref, a_ref, tile_ref,
):
    step = pl.program_id(0)
    seq = x_ref.shape[0]
    width = wq_ref.shape[1]

    @pl.when(step == 0)
    def _():
        unit, _inv = unit_rows(x_ref[...].astype(F32))
        a_ref[...] = (unit * gain_ref[...]).astype(BF16)

    for w_ref, out_ref in ((wq_ref, q_ref), (wk_ref, k_ref), (wv_ref, v_ref)):
        out_ref[...] = nn(a_ref[...], w_ref[...]).astype(BF16)

    key_pos = lax.broadcasted_iota(jnp.int32, (seq, 1), 0)
    key_dead = key_pos >= length_ref[0]
    row = lax.broadcasted_iota(jnp.int32, (ROWS, ROWS + LANES), 0)
    col = lax.broadcasted_iota(jnp.int32, (ROWS, ROWS + LANES), 1)
    ahead = col - LANES > row
    for pair in range(width // LANES):
        cols = slice(pair * LANES, (pair + 1) * LANES)
        outs = [None] * (seq // ROWS)
        for which in range(2):
            local = pair * 2 + which
            head = step * (width // DH) + local
            spun = pltpu.roll(
                jnp.broadcast_to(near_ref[pl.ds(head, 1), :], (ROWS, 4 * LANES)),
                0, 1, stride=1, stride_axis=0,
            )
            tile_ref[...] = jnp.where(ahead, MASKED, spun[:, : ROWS + LANES])
            own = head_lane((seq, LANES), which)
            extra = lax.broadcasted_iota(jnp.int32, (seq, LANES), 1) == (DH if which == 0 else 0)
            far = jnp.where(key_dead, MASKED, far_ref[head]).astype(BF16)
            keys = jnp.where(own, k_ref[:, cols], jnp.where(extra, far, jnp.zeros((), BF16)))
            values = jnp.where(own, v_ref[:, cols], jnp.zeros((), BF16))
            queries = jnp.where(own, q_ref[:, cols], jnp.where(extra, 1.0, 0.0).astype(BF16))
            for blk in range(seq // ROWS):
                rows = slice(blk * ROWS, (blk + 1) * ROWS)
                span = (blk + 1) * ROWS
                cut = max(span - ROWS - LANES, 0)
                scores = nt(queries[rows], keys[:span])
                if cut:
                    near = scores[:, cut:] + tile_ref[...]
                    scores = jnp.concatenate([scores[:, :cut], near], axis=1)
                elif span == ROWS:
                    scores = scores + tile_ref[:, LANES:]
                else:
                    near = scores[:, ROWS - LANES :] + tile_ref[...]
                    scores = jnp.concatenate([scores[:, : ROWS - LANES], near], axis=1)
                top = jnp.max(scores, axis=1, keepdims=True)
                weights = jnp.exp(scores - top)
                total = jnp.sum(weights, axis=1, keepdims=True)
                probs = (weights * (1.0 / total)).astype(BF16)
                p_ref[local, rows, :span] = probs
                mixed = nn(probs, values[:span])
                outs[blk] = mixed if outs[blk] is None else outs[blk] + mixed
        for blk in range(seq // ROWS):
            o_ref[blk * ROWS : (blk + 1) * ROWS, cols] = outs[blk].astype(BF16)


def self_forward(length, x, gain, wq, wk, wv, far, near):
    seq, model = x.shape
    width = 256
    steps = model // width
    whole = lambda shape: pl.BlockSpec(shape, lambda i: (0,) * len(shape))
    smem = pl.BlockSpec(memory_space=pltpu.SMEM)
    columns = pl.BlockSpec((seq, width), lambda i: (0, i))
    weight = pl.BlockSpec((model, width), lambda i: (0, i))
    heads = width // DH
    return pl.pallas_call(
        self_forward_kernel,
        grid=(steps,),
        in_specs=[
            smem, whole((seq, model)), whole((1, model)), weight, weight, weight,
            smem, whole(near.shape),
        ],
        out_specs=[
            columns, columns, columns, columns,
            pl.BlockSpec((heads, seq, seq), lambda i: (i, 0, 0)),
            whole((seq, model)),
        ],
        out_shape=[jax.ShapeDtypeStruct((seq, model), BF16)] * 4
        + [
            jax.ShapeDtypeStruct((H, seq, seq), BF16),
            jax.ShapeDtypeStruct((seq, model), BF16),
        ],
        scratch_shapes=[pltpu.VMEM((ROWS, ROWS + LANES), F32)],
        compiler_params=pltpu.CompilerParams(vmem_limit_bytes=60 * 1024 * 1024),
        cost_estimate=pl.CostEstimate(
            flops=6 * seq * model * model + 4 * seq * seq * model,
            bytes_accessed=2 * H * seq * seq + 16 * seq * model,
            transcendentals=H * seq * seq,
        ),
        name="self_forward",
    )(length, x, gain, wq, wk, wv, far, near)


def middle_kernel(
    length_ref, x_ref, o_ref, cot_ref, enc_ref, gain_ref, wo_ref, cq_ref, ck_ref, cv_ref,
    co_ref, win_ref, wdown_ref,
    out_ref, g1_ref, a2_ref, mix_ref, a3_ref, r_ref, du_ref, g_ref, g2_ref, dcq_ref,
    dck_ref, dcv_ref, egrad_ref, gain_grad_ref,
    keys_ref, values_ref, dk_acc, dv_acc,
):
    step = pl.program_id(0)
    last = pl.num_programs(0) - 1
    rows = x_ref.shape[0]
    model = x_ref.shape[1]
    pairs = model // LANES

    @pl.when(step == 0)
    def _():
        keys_ref[...] = nn(enc_ref[...], ck_ref[...]).astype(BF16)
        values_ref[...] = nn(enc_ref[...], cv_ref[...]).astype(BF16)
        dk_acc[...] = jnp.zeros_like(dk_acc)
        dv_acc[...] = jnp.zeros_like(dv_acc)
        gain_grad_ref[...] = jnp.zeros_like(gain_grad_ref)

    gain_cross = gain_ref[0:1, :]
    gain_ffn = gain_ref[1:2, :]
    pos = step * rows + lax.broadcasted_iota(jnp.int32, (rows, 1), 0)
    valid = jnp.where(pos < length_ref[0], 1.0, 0.0).astype(F32)

    x1 = x_ref[...].astype(F32) + nn(o_ref[...], wo_ref[...])
    unit2, inv2 = unit_rows(x1)
    a2 = (unit2 * gain_cross).astype(BF16)
    a2_ref[...] = a2
    cq = nn(a2, cq_ref[...]).astype(BF16)
    probs = []
    mixed = []
    zero = jnp.zeros((), BF16)
    for pair in range(pairs):
        cols = slice(pair * LANES, (pair + 1) * LANES)
        total_out = None
        for which in range(2):
            own = head_lane((rows, LANES), which)
            own_key = head_lane((keys_ref.shape[0], LANES), which)
            scores = nt(jnp.where(own, cq[:, cols], zero), keys_ref[:, cols])
            top = jnp.max(scores, axis=1, keepdims=True)
            weights = jnp.exp(scores - top)
            prob = weights * (1.0 / jnp.sum(weights, axis=1, keepdims=True))
            probs.append(prob)
            part = nn(prob.astype(BF16), jnp.where(own_key, values_ref[:, cols], zero))
            total_out = part if total_out is None else total_out + part
        mixed.append(total_out.astype(BF16))
    mix = jnp.concatenate(mixed, axis=1)
    mix_ref[...] = mix
    x2 = x1 + nn(mix, co_ref[...])
    unit3, inv3 = unit_rows(x2)
    a3 = (unit3 * gain_ffn).astype(BF16)
    a3_ref[...] = a3
    grad = cot_ref[...].astype(F32) * valid
    grad_low = grad.astype(BF16)
    g_ref[...] = grad_low
    result = x2
    dy3 = None
    hidden_count = win_ref.shape[0]
    chunk = model
    for start in range(0, hidden_count, chunk):
        part = slice(start, start + chunk)
        z = nt(a3, win_ref[part, :])
        zz = z * z
        t = jnp.tanh(GELU_C * z * (1.0 + GELU_A * zz))
        half = 0.5 + 0.5 * t
        r = (z * half).astype(BF16)
        r_ref[:, part] = r
        slope = half + (0.5 * GELU_C) * z * (1.0 - t * t) * (1.0 + (3.0 * GELU_A) * zz)
        du = (nt(grad_low, wdown_ref[part, :]) * slope).astype(BF16)
        du_ref[:, part] = du
        result = result + nn(r, wdown_ref[part, :])
        back = nn(du, win_ref[part, :])
        dy3 = back if dy3 is None else dy3 + back
    out_ref[...] = result * valid
    through, gain_part = norm_back(dy3, unit3, inv3, gain_ffn)
    gain_grad_ref[1:2, :] += gain_part
    g2 = grad + through
    g2_low = g2.astype(BF16)
    g2_ref[...] = g2_low
    dmix = nt(g2_low, co_ref[...]).astype(BF16)
    dq_parts = []
    for pair in range(pairs):
        cols = slice(pair * LANES, (pair + 1) * LANES)
        dq = None
        for which in range(2):
            own = head_lane((rows, LANES), which)
            own_key = head_lane((keys_ref.shape[0], LANES), which)
            prob = probs[2 * pair + which]
            d_out = jnp.where(own, dmix[:, cols], zero)
            dp = nt(d_out, values_ref[:, cols])
            ds = prob * (dp - jnp.sum(prob * dp, axis=1, keepdims=True))
            ds_low = ds.astype(BF16)
            dv_acc[:, cols] += tn(prob.astype(BF16), d_out)
            dk_acc[:, cols] += tn(ds_low, jnp.where(own, cq[:, cols], zero))
            part = nn(ds_low, jnp.where(own_key, keys_ref[:, cols], zero))
            dq = part if dq is None else dq + part
        dq_parts.append(dq.astype(BF16))
    dcq = jnp.concatenate(dq_parts, axis=1)
    dcq_ref[...] = dcq
    through, gain_part = norm_back(nt(dcq, cq_ref[...]), unit2, inv2, gain_cross)
    gain_grad_ref[0:1, :] += gain_part
    g1_ref[...] = g2 + through

    @pl.when(step == last)
    def _():
        dk = dk_acc[...].astype(BF16)
        dv = dv_acc[...].astype(BF16)
        dck_ref[...] = dk
        dcv_ref[...] = dv
        egrad_ref[...] = nt(dk, ck_ref[...]) + nt(dv, cv_ref[...])


def middle(length, x, o, cot, enc, gains, wo, cq, ck, cv, co, win_t, wdown):
    seq, model = x.shape
    hidden = win_t.shape[0]
    enc_len = enc.shape[0]
    steps = seq // ROWS
    whole = lambda shape: pl.BlockSpec(shape, lambda i: (0,) * len(shape))
    held = lambda shape: pl.BlockSpec(
        shape, lambda i: (0,) * len(shape), pipeline_mode=pl.Buffered(1)
    )
    smem = pl.BlockSpec(memory_space=pltpu.SMEM)
    block = lambda width: pl.BlockSpec((ROWS, width), lambda i: (i, 0))
    square = held((model, model))
    wide = held((hidden, model))
    low = lambda width: jax.ShapeDtypeStruct((seq, width), BF16)
    return pl.pallas_call(
        middle_kernel,
        grid=(steps,),
        in_specs=[
            smem, block(model), block(model), block(model), held((enc_len, model)),
            held((2, model)), square, square, square, square, square, wide, wide,
        ],
        out_specs=[
            block(model), block(model), block(model), block(model), block(model),
            block(hidden), block(hidden), block(model), block(model), block(model),
            whole((enc_len, model)), whole((enc_len, model)), whole((enc_len, model)),
            whole((2, model)),
        ],
        out_shape=[
            jax.ShapeDtypeStruct((seq, model), F32),
            jax.ShapeDtypeStruct((seq, model), F32),
            low(model), low(model), low(model), low(hidden), low(hidden),
            low(model), low(model), low(model),
            jax.ShapeDtypeStruct((enc_len, model), BF16),
            jax.ShapeDtypeStruct((enc_len, model), BF16),
            jax.ShapeDtypeStruct((enc_len, model), F32),
            jax.ShapeDtypeStruct((2, model), F32),
        ],
        scratch_shapes=[
            pltpu.VMEM((enc_len, model), BF16),
            pltpu.VMEM((enc_len, model), BF16),
            pltpu.VMEM((enc_len, model), F32),
            pltpu.VMEM((enc_len, model), F32),
        ],
        compiler_params=pltpu.CompilerParams(vmem_limit_bytes=60 * 1024 * 1024),
        cost_estimate=pl.CostEstimate(
            flops=12 * seq * model * model + 8 * seq * model * hidden,
            bytes_accessed=40 * seq * model + 10 * model * model + 4 * hidden * model,
            transcendentals=seq * hidden,
        ),
        name="middle",
    )(length, x, o, cot, enc, gains, wo, cq, ck, cv, co, win_t, wdown)


def self_backward_kernel(
    x_ref, gain_ref, a_ref, g1_ref, q_ref, k_ref, v_ref, o_ref, p_ref,
    wo_ref, wq_ref, wk_ref, wv_ref,
    ingrad_ref, gwq_ref, gwk_ref, gwv_ref, gwo_ref, gain_grad_ref, hist_ref,
    low_ref, dy_acc, near_acc, dk_acc, dv_acc, dq_scr,
):
    step = pl.program_id(0)
    last = pl.num_programs(0) - 1
    seq = x_ref.shape[0]
    width = wq_ref.shape[1]

    @pl.when(step == 0)
    def _():
        low_ref[...] = g1_ref[...].astype(BF16)
        dy_acc[...] = jnp.zeros_like(dy_acc)

    d_all = nt(low_ref[...], wo_ref[...]).astype(BF16)
    gwo_ref[...] = tn(o_ref[...], low_ref[...]).astype(BF16)
    zero = jnp.zeros((), BF16)
    for pair in range(width // LANES):
        cols = slice(pair * LANES, (pair + 1) * LANES)
        dk_acc[...] = jnp.zeros_like(dk_acc)
        dv_acc[...] = jnp.zeros_like(dv_acc)
        dq_blocks = [None] * (seq // ROWS)
        for which in range(2):
            local = pair * 2 + which
            head = step * (width // DH) + local
            own = head_lane((seq, LANES), which)
            d_out = jnp.where(own, d_all[:, cols], zero)
            queries = jnp.where(own, q_ref[:, cols], zero)
            keys = jnp.where(own, k_ref[:, cols], zero)
            for blk in range(seq // ROWS):
                rows = slice(blk * ROWS, (blk + 1) * ROWS)
                span = (blk + 1) * ROWS
                prob_low = p_ref[local, rows, :span]
                prob = prob_low.astype(F32)
                dp = nt(d_out[rows], v_ref[:span, cols])
                ds = prob * (dp - jnp.sum(prob * dp, axis=1, keepdims=True))
                if blk == 0:
                    near_acc[:, :LANES] = jnp.zeros((ROWS, LANES), F32)
                    near_acc[:, LANES:] = ds
                else:
                    near_acc[...] += ds[:, span - ROWS - LANES :]
                ds_low = ds.astype(BF16)
                part = nn(ds_low, keys[:span])
                dq_blocks[blk] = part if which == 0 else dq_blocks[blk] + part
                dk_acc[:span, :] += tn(ds_low, queries[rows])
                dv_acc[:span, :] += tn(prob_low, d_out[rows])
            padded = jnp.concatenate(
                [near_acc[...], jnp.zeros((ROWS, LANES), F32)], axis=1
            )
            count = ROWS
            while count > 1:
                count //= 2
                padded = padded[:count] + pltpu.roll(padded[count:], 4 * LANES - count, 1)
            hist_ref[pl.ds(head, 1), :] = padded
        for blk in range(seq // ROWS):
            rows = slice(blk * ROWS, (blk + 1) * ROWS)
            dq_scr[0, rows, cols] = dq_blocks[blk].astype(BF16)
        dq_scr[1, :, cols] = dk_acc[...].astype(BF16)
        dq_scr[2, :, cols] = dv_acc[...].astype(BF16)
    dy_acc[...] += (
        nt(dq_scr[0], wq_ref[...]) + nt(dq_scr[1], wk_ref[...]) + nt(dq_scr[2], wv_ref[...])
    )
    gwq_ref[...] = tn(a_ref[...], dq_scr[0]).astype(BF16)
    gwk_ref[...] = tn(a_ref[...], dq_scr[1]).astype(BF16)
    gwv_ref[...] = tn(a_ref[...], dq_scr[2]).astype(BF16)

    @pl.when(step == last)
    def _():
        unit, inv = unit_rows(x_ref[...].astype(F32))
        through, gain_part = norm_back(dy_acc[...], unit, inv, gain_ref[...])
        ingrad_ref[...] = g1_ref[...] + through
        gain_grad_ref[...] = gain_part


def self_backward(x, gain, a1, g1, q, k, v, o, p, wo, wq, wk, wv):
    seq, model = x.shape
    width = 256
    heads = width // DH
    steps = model // width
    held = lambda shape: pl.BlockSpec(
        shape, lambda i: (0,) * len(shape), pipeline_mode=pl.Buffered(1)
    )
    whole = lambda shape: pl.BlockSpec(shape, lambda i: (0,) * len(shape))
    columns = pl.BlockSpec((seq, width), lambda i: (0, i))
    weight = pl.BlockSpec((model, width), lambda i: (0, i))
    weight_rows = pl.BlockSpec((width, model), lambda i: (i, 0))
    square = jax.ShapeDtypeStruct((model, model), BF16)
    return pl.pallas_call(
        self_backward_kernel,
        grid=(steps,),
        in_specs=[
            held((seq, model)), held((1, model)), held((seq, model)), held((seq, model)),
            columns, columns, columns, columns,
            pl.BlockSpec((heads, seq, seq), lambda i: (i, 0, 0)),
            weight_rows, weight, weight, weight,
        ],
        out_specs=[
            whole((seq, model)), weight, weight, weight, weight_rows, whole((1, model)),
            whole((16, 4 * LANES)),
        ],
        out_shape=[
            jax.ShapeDtypeStruct((seq, model), F32), square, square, square, square,
            jax.ShapeDtypeStruct((1, model), F32),
            jax.ShapeDtypeStruct((16, 4 * LANES), F32),
        ],
        scratch_shapes=[
            pltpu.VMEM((seq, model), BF16),
            pltpu.VMEM((seq, model), F32),
            pltpu.VMEM((ROWS, ROWS + LANES), F32),
            pltpu.VMEM((seq, LANES), F32),
            pltpu.VMEM((seq, LANES), F32),
            pltpu.VMEM((3, seq, width), BF16),
        ],
        compiler_params=pltpu.CompilerParams(vmem_limit_bytes=60 * 1024 * 1024),
        cost_estimate=pl.CostEstimate(
            flops=16 * seq * model * model + 8 * seq * seq * model,
            bytes_accessed=2 * H * seq * seq + 24 * seq * model,
            transcendentals=0,
        ),
        name="self_backward",
    )(x, gain, a1, g1, q, k, v, o, p, wo, wq, wk, wv)


def body(
    tokens, encoder_states, lengths, dealing, cotangent,
    w_query, w_key, w_value, w_out, c_query, c_key, c_value, c_out, w_in, w_down,
    gain_self, gain_cross, gain_ffn, bias_table,
):
    axes = ("dp", "fsdp")
    fsdp_size = lax.axis_size("fsdp")
    dp_size = lax.axis_size("dp")
    dev_count = dp_size * fsdp_size
    dp_index = lax.axis_index("dp")
    own = dp_index * fsdp_size + lax.axis_index("fsdp")
    seq_len, model = tokens.shape[1:]
    route = [(a, a ^ 1) for a in range(dp_size)]

    x = tokens[0]
    cot = cotangent[0]
    in_place = lax.dynamic_slice_in_dim(dealing, own, 1) == own
    enc_other = lax.ppermute(encoder_states[0], "dp", route)
    enc = jnp.where(in_place[:, None], encoder_states[0], enc_other)
    length = lax.dynamic_slice_in_dim(lengths, own, 1)

    part = w_query.shape[0]
    gain_part = gain_self.shape[0]
    small = jnp.concatenate([gain_self, gain_cross, gain_ffn, bias_table])
    small_row = jnp.pad(small, (0, model - small.shape[0]))[None, :]
    small_row = jnp.pad(small_row, ((0, 7), (0, 0)))
    first = lax.all_gather(
        jnp.concatenate([w_query, w_key, w_value, small_row], axis=0), axes, axis=0
    )
    second = lax.all_gather(
        jnp.concatenate([w_out, c_query, c_key, c_value, c_out, w_in.T, w_down], axis=0),
        axes, axis=0,
    )
    square = lambda pile, at: pile[:, at * part : (at + 1) * part].reshape(-1, model)
    wq, wk, wv = (square(first, i) for i in range(3))
    wo, cq, ck, cv, co = (square(second, i) for i in range(5))
    ff_part = w_down.shape[0]
    win_t = second[:, 5 * part : 5 * part + ff_part].reshape(-1, model)
    wdown = second[:, 5 * part + ff_part :].reshape(-1, model)
    small_all = first[:, 3 * part].astype(F32)
    gains = [
        small_all[:, i * gain_part : (i + 1) * gain_part].reshape(1, model) for i in range(3)
    ]
    table_part = bias_table.shape[0]
    table = small_all[:, 3 * gain_part : 3 * gain_part + table_part].reshape(NB, H)

    distance = jnp.arange(LANES + 1, dtype=jnp.int32)
    bucket_hot = (bucket_of(distance)[:, None] == jnp.arange(NB, dtype=jnp.int32)[None, :]).astype(
        F32
    )
    by_distance = jnp.dot(bucket_hot, table, precision=lax.Precision.HIGHEST)
    far = by_distance[LANES]
    near = (by_distance - far[None, :])[::-1].T
    near = jnp.pad(near, ((0, 16 - H), (0, 4 * LANES - near.shape[1])))

    q, k, v, o, p, a1 = self_forward(length, x, gains[0], wq, wk, wv, far, near)
    (
        out, g1, a2, mix, a3, r, du, g_low, g2_low, dcq, dck, dcv, egrad, mid_gain_grad,
    ) = middle(
        length, x, o, cot, enc, jnp.concatenate(gains[1:], axis=0),
        wo, cq, ck, cv, co, win_t, wdown,
    )
    split = lambda grad: grad.reshape(dev_count, -1, model)
    g_down = tn(r, g_low).astype(BF16)
    g_in = tn(du, a3).astype(BF16)
    g_cq = tn(a2, dcq).astype(BF16)
    g_co = tn(mix, g2_low).astype(BF16)
    g_ck = tn(enc, dck).astype(BF16)
    g_cv = tn(enc, dcv).astype(BF16)
    pile_one = jnp.concatenate(
        [split(g) for g in (g_cq, g_ck, g_cv, g_co, g_in, g_down)], axis=1
    )
    sum_one = lax.psum_scatter(pile_one, axes, scatter_dimension=0, tiled=False).astype(F32)

    in_grad, g_wq, g_wk, g_wv, g_wo, self_gain_grad, hist = self_backward(
        x, gains[0], a1, g1, q, k, v, o, p, wo, wq, wk, wv
    )
    by_dist = hist[:H, :LANES][:, ::-1]
    by_dist = jnp.concatenate([hist[:H, LANES : LANES + 1], by_dist[:, : LANES - 1]], axis=1)
    near_hot = bucket_hot[:LANES] * (jnp.arange(NB) < NB - 1).astype(F32)
    near_sums = jnp.dot(near_hot.T, by_dist.T, precision=lax.Precision.HIGHEST)
    grad_table = jnp.where(
        (jnp.arange(NB) < NB - 1)[:, None],
        near_sums, -jnp.sum(near_sums, axis=0, keepdims=True),
    )
    small_grads = jnp.concatenate(
        [
            self_gain_grad.reshape(dev_count, -1),
            mid_gain_grad[0].reshape(dev_count, -1),
            mid_gain_grad[1].reshape(dev_count, -1),
            grad_table.reshape(dev_count, -1),
        ],
        axis=1,
    )
    low = small_grads.astype(BF16)
    rest = (small_grads - low.astype(F32)).astype(BF16)
    both = jnp.concatenate([low, rest], axis=1)
    both = jnp.pad(both, ((0, 0), (0, model - both.shape[1])))[:, None, :]
    pile_two = jnp.concatenate(
        [split(g) for g in (g_wq, g_wk, g_wv, g_wo)] + [jnp.pad(both, ((0, 0), (0, 7), (0, 0)))],
        axis=1,
    )
    sum_two = lax.psum_scatter(pile_two, axes, scatter_dimension=0, tiled=False).astype(F32)

    egrad_other = lax.ppermute(egrad, "dp", route)
    encoder_grad = jnp.where(in_place[:, None], egrad, egrad_other)
    rows_of = lambda pile, at: pile[at * part : (at + 1) * part]
    ends = sum_two[4 * part]
    small_count = small_grads.shape[1]
    ends = ends[:small_count] + ends[small_count : 2 * small_count]
    return (
        out[None], in_grad[None], encoder_grad[None],
        rows_of(sum_two, 0), rows_of(sum_two, 1), rows_of(sum_two, 2), rows_of(sum_two, 3),
        rows_of(sum_one, 0), rows_of(sum_one, 1), rows_of(sum_one, 2), rows_of(sum_one, 3),
        sum_one[4 * part : 4 * part + ff_part].T,
        sum_one[4 * part + ff_part :],
        ends[:gain_part], ends[gain_part : 2 * gain_part], ends[2 * gain_part : 3 * gain_part],
        ends[3 * gain_part :],
    )


def solution(mesh):
    rows3 = P(("dp", "fsdp"), None, None)
    rows2 = P(("dp", "fsdp"), None)
    cols2 = P(None, ("dp", "fsdp"))
    line = P(("dp", "fsdp"))
    in_specs = (
        (rows3, rows3, P(), P(), rows3) + (rows2,) * 8 + (cols2, rows2) + (line,) * 4
    )
    out_specs = (rows3,) * 3 + (rows2,) * 8 + (cols2, rows2) + (line,) * 4
    return jax.shard_map(body, mesh=mesh, in_specs=in_specs, out_specs=out_specs, check_vma=False)
```

time: 4310 us -> 611 us (0.14)
  local copies, waits for them, and re-layouts: 3010 us -> 55.3 us
  waiting for transfers between devices: 769 us -> 369 us
  matrix products: 279 us -> 15.5 us
  Pallas kernels: 0 us -> 137 us
  blocking collectives: 129 us -> 0 us
  other arithmetic: 91.7 us -> 6.94 us
    gather x5 -> x0, local copies, waits for them, and re-layouts: 2800 us -> none  [the longest x4 2800 us: score_block(): near_bias = jnp.take(bias_dist, jnp.maximum(distance, 0), axis=1)]
    reduce_scatter x8 -> x2, waiting for transfers between devices: 555 us -> 231 us  [the longest x1 166 us: body(): lax.psum_scatter(pile_one, axes, scatter_dimension=0, tiled=False)]
    dot_general x56 -> x8, matrix products: 279 us -> 15.5 us  [the longest x6 15 us: tn(): lax.dot_general(left_op, right_op, (((0,), (0,)), ((), ())), preferred_el...]
    unnamed x22 -> x4, waiting for transfers between devices: 214 us -> 0.07 us
    pallas_call x0 -> x3, Pallas kernels: none -> 137 us  [the longest x1 58.2 us: middle(): pl.pallas_call(middle_kernel, grid=(steps,), in_specs=[smem, block(model)...]
    unnamed x2 -> x0, blocking collectives: 129 us -> none
    all_gather x10 -> x2, waiting for transfers between devices: 0.07 us -> 124 us  [the longest x1 73.5 us: body(): lax.all_gather(jnp.concatenate([w_out, c_query, c_key, c_value, c_out, w_...]
    reshape x6 -> x4, local copies, waits for them, and re-layouts: 75.5 us -> 0.93 us  [the longest x3 0.85 us: body(): small_all[:, i * gain_part:(i + 1) * gain_part].reshape(1, model)]
  transfers between devices with their start and end apart: 24 -> 6, of which waited for: 7 -> 6; matrix products, arithmetic and copies ran while one was open for 75% -> 7% of each run, Pallas kernels for 0% -> 5%
where the time goes in v1:
time: 611 us; the launch traced here: 603 us
  waiting for transfers between devices  369 us (60%)
  Pallas kernels  137 us (22%)
  local copies, waits for them, and re-layouts  55.3 us (9%)
  matrix products  15.5 us (3%)
  between operations  15 us (2%)
  other arithmetic  6.94 us (1%)
    reduce_scatter x1, waiting for transfers between devices, body(): lax.psum_scatter(pile_one, axes, scatter_dimension=0, tiled=False)  166 us
    all_gather x1, waiting for transfers between devices, body(): lax.all_gather(jnp.concatenate([w_out, c_query, c_key, c_value, c_out, w_...  73.5 us
    reduce_scatter x1, waiting for transfers between devices, body(): lax.psum_scatter(pile_two, axes, scatter_dimension=0, tiled=False)  65.2 us
    pallas_call x1, Pallas kernels, middle(): pl.pallas_call(middle_kernel, grid=(steps,), in_specs=[smem, block(model)...  58.2 us
    all_gather x1, waiting for transfers between devices, body(): lax.all_gather(jnp.concatenate([w_query, w_key, w_value, small_row], axis...  50.5 us
    pallas_call x1, Pallas kernels, self_backward(): pl.pallas_call(self_backward_kernel, grid=(steps,), in_specs=[held((seq,...  49.9 us
    pallas_call x1, Pallas kernels, self_forward(): pl.pallas_call(self_forward_kernel, grid=(steps,), in_specs=[smem, whole(...  29.2 us
    unnamed x64, local copies, waits for them, and re-layouts  24.4 us
  transfers between devices with their start and end apart: 6, of which 6 were waited for; matrix products, arithmetic and copies ran while one was open for 7% of the time, Pallas kernels for 5%

profile of v1, /device:TPU:0, one launch (start us, length us, event | category | flops | bytes accessed | tf_op | source)
XLA Modules:
  0.0 602.9 jit_solution(10706460800041699927)
XLA Ops:
  8.1 1.5 fusion.1
  16.2 3.1 collective-permute-start
  21.3 2.9 collective-permute-done
  24.9 50.5 %all-gather.5.cloned.1.call-done = bf16[2560,768]{1,0:T(8,128)(2,1)} async-done(((bf16[80,768]{1,0:T(8,128)(2,1)}), bf16[2560,768]{1,0:T(8,128)(2,1)}) %all-gather.5.cloned.1.call-update) | async-done | bytes 3932176 | tf_op jit(solution)/shard_map/all_gather | solution.py:487
  75.4 1.0 slice.216
  79.3 3.9 fusion.58
  83.3 29.2 %self_forward.1 = (bf16[1024,768]{1,0:T(8,128)(2,1)}, bf16[1024,768]{1,0:T(8,128)(2,1)}, bf16[1024,768]{1,0:T(8,128)(2,1)}, bf16[1024,768]{1,0:T(8,128)(2,1)}, b...) custom-call(s32[1]{0:T(128)} %dynamic_slice.6.length_ref, bf16[1024,768]{1,0:T(8,128)(2,1)} %bitcast.119, ...), custom_call_target="tpu_custom_call" | custom-call | flops 6845104128 | bytes 37748736 | tf_op jit(solution)/shard_map/self_forward/pallas_call | solution.py:141
  112.4 73.5 %all-gather.7.cloned.1.call-done = bf16[9984,768]{1,0:T(8,128)(2,1)} async-done(((bf16[312,768]{1,0:T(8,128)(2,1)}), bf16[9984,768]{1,0:T(8,128)(2,1)}) %all-gather.7.cloned.1.call-update) | async-done | bytes 15335440 | tf_op jit(solution)/shard_map/all_gather | solution.py:490
  185.9 5.4 fusion.57
  191.3 8.0 %fusion.56 = (bf16[32,96,768]{2,1,0:T(8,128)(2,1)}, bf16[32,96,768]{2,1,0:T(8,128)(2,1)}) fusion(bf16[32,312,768]{2,1,0:T(8,128)(2,1)} %bitcast.87), kind=kLoop, calls=%fused_computation.128 | loop fusion | bytes 18874368 | tf_op jit(solution)/shard_map/slice | solution.py:499
  199.3 58.2 %middle.1 = (f32[1024,768]{1,0:T(8,128)}, f32[1024,768]{1,0:T(8,128)}, bf16[1024,768]{1,0:T(8,128)(2,1)}, bf16[1024,768]{1,0:T(8,128)(2,1)}, bf16[1024,768]{1,0:...) custom-call(s32[1]{0:T(128)} %dynamic_slice.6.length_ref, ...), custom_call_target="tpu_custom_call" | custom-call | flops 26575110144 | bytes 46792704 | tf_op jit(solution)/shard_map/middle/pallas_call | solution.py:297
  257.5 49.9 %self_backward.1 = (f32[1024,768]{1,0:T(8,128)}, bf16[768,768]{1,0:T(8,128)(2,1)}, bf16[768,768]{1,0:T(8,128)(2,1)}, bf16[768,768]{1,0:T(8,128)(2,1)}, bf16[768,...) custom-call(bf16[1024,768]{1,0:T(8,128)(2,1)} %bitcast.121, f32[1,768]{1,0:T(1,128)} %reshape.203.gain_ref, ...), custom_call_target="tpu_custom_call" | custom-call | flops 16106127360 | bytes 44040192 | tf_op jit(solution)/shard_map/self_backward/pallas_call | solution.py:425
  309.1 2.4 constant_dynamic-update-slice_fusion.9
  312.6 1.1 constant_dynamic-update-slice_fusion.8
  313.8 1.2 constant_dynamic-update-slice_fusion.7
  315.5 1.1 constant_dynamic-update-slice_fusion.6
  317.5 1.3 copy-done.16
  319.3 1.4 convolution_convert_fusion.5
  320.8 1.1 constant_dynamic-update-slice_fusion.15
  322.5 1.1 constant_dynamic-update-slice_fusion.14
  324.1 1.1 constant_dynamic-update-slice_fusion.13
  326.1 1.5 convolution_convert_fusion.2
  327.6 1.1 constant_dynamic-update-slice_fusion.12
  330.2 5.5 convolution_convert_fusion.1
  335.8 2.5 constant_dynamic-update-slice_fusion.11
  338.3 5.6 convolution_convert_fusion
  343.9 2.5 constant_dynamic-update-slice_fusion.10
  346.4 1.0 copy-done.5
  347.9 10.8 %collective-permute-done.1 = f32[128,768]{1,0:T(8,128)S(1)} collective-permute-done((f32[128,768]{1,0:T(8,128)S(1)}, f32[128,768]{1,0:T(8,128)S(1)}, u32[]{:S(2)}, u32[]{:S(2)}) %collective-permute-start.1) | collective-permute-done | bytes 393248 | tf_op jit(solution)/shard_map/ppermute | solution.py:565
  359.5 65.2 %reduce-scatter.3.cloned.1.call-done = bf16[1,104,768]{2,1,0:T(8,128)(2,1)} async-done(((bf16[32,104,768]{2,1,0:T(8,128)(2,1)}), bf16[1,104,768]{2,1,0:T(8,128)(2,1)}) %reduce-scatter.3.cloned.1.call-update) | async-done | bytes 159760 | tf_op jit(solution)/shard_map/reduce_scatter | solution.py:563
  427.6 166.0 %reduce-scatter.5.cloned.1.call-done = bf16[1,288,768]{2,1,0:T(8,128)(2,1)} async-done(((bf16[32,288,768]{2,1,0:T(8,128)(2,1)}), bf16[1,288,768]{2,1,0:T(8,128)(2,1)}) %reduce-scatter.5.cloned.1.call-update) | async-done | bytes 442384 | tf_op jit(solution)/shard_map/reduce_scatter | solution.py:533
  593.6 1.1 convert_element_type.220
  (108 shorter events, 26.1 us)
Async XLA Ops:
  7.2 9.0 %copy-start.8 = (bf16[1,128,768]{2,1,0:T(8,128)(2,1)S(1)}, bf16[1,128,768]{2,1,0:T(8,128)(2,1)}, u32[]{:S(2)}) copy-start(bf16[1,128,768]{2,1,0:T(8,128)(2,1)} %param.20) | copy-start | bytes 589828
  7.2 12.1 %copy-start.12 = (s32[32]{0:T(128)S(1)}, s32[32]{0:T(128)}, u32[]{:S(2)}) copy-start(s32[32]{0:T(128)} %param.21) | copy-start | bytes 388
  7.2 12.7 %copy-start.13 = (s32[32]{0:T(128)S(1)}, s32[32]{0:T(128)}, u32[]{:S(2)}) copy-start(s32[32]{0:T(128)} %param.22) | copy-start | bytes 388
  7.2 68.2 %all-gather.5.cloned.1.call-start = ((), (), s32[]{:S(2)}) async-start(), calls=%async_computation.4 | async-start | bytes 4055040 | tf_op jit(solution)/shard_map/all_gather | solution.py:487
  9.6 176.3 %all-gather.7.cloned.1.call-start = ((), (), s32[]{:S(2)}) async-start(), calls=%async_computation.5 | async-start | bytes 15814656 | tf_op jit(solution)/shard_map/all_gather | solution.py:490
  15.4 0.8 copy-start.4
  16.2 408.5 %reduce-scatter.3.cloned.1.call-start = ((), (), s32[]{:S(2)}) async-start(), calls=%async_computation.2 | async-start | bytes 5271552 | tf_op jit(solution)/shard_map/reduce_scatter | solution.py:563
  16.2 8.0 %collective-permute-start = (bf16[128,768]{1,0:T(8,128)(2,1)S(1)}, bf16[128,768]{1,0:T(8,128)(2,1)S(1)}, u32[]{:S(2)}, u32[]{:S(2)}) collective-permute-start(bf16[128,768]{1,0:T(8,128)(2,1)S(1)} %bitcast.116), channel_id=1, source_target_pairs={{0,8},{8,0},{16,24},{24,16},{1,9},{9,1},{17,25},{25,17},{2,10},{10... | collective-permute-start | bytes 589832 | tf_op jit(solution)/shard_map/ppermute | solution.py:478
  77.6 5.6 copy-start.11
  307.5 4.6 copy-start.9
  307.5 4.8 copy-start.10
  307.5 5.1 copy-start.3
  311.5 2.3 copy-start.2
  313.8 1.7 copy-start.1
  317.4 1.4 copy-start.16
  317.4 1.9 copy-start.17
  317.5 276.2 %reduce-scatter.5.cloned.1.call-start = ((), (), s32[]{:S(2)}) async-start(), calls=%async_computation.3 | async-start | bytes 14598144 | tf_op jit(solution)/shard_map/reduce_scatter | solution.py:533
  320.8 1.2 copy-start
  320.8 1.2 copy-start.7
  322.5 1.2 copy-start.6
  323.6 1.6 copy-start.15
  324.1 2.0 copy-start.14
  326.1 3.4 copy-start.18
  327.6 2.6 copy-start.20
  327.6 10.6 %slice-start = ((s8[6291456]{0:T(1024)(128)(4,1)}), s8[4194304]{0:T(1024)(128)(4,1)S(1)}, s32[]{:S(2)}) async-start(s8[6291456]{0:T(1024)(128)(4,1)} %bitcast.124), calls=%async_computation.6 | async-start | bytes 8388608
  330.2 8.0 %slice-start.1 = ((s8[6291456]{0:T(1024)(128)(4,1)}), s8[2097152]{0:T(1024)(128)(4,1)S(1)}, s32[]{:S(2)}) async-start(s8[6291456]{0:T(1024)(128)(4,1)} %bitcast.124), calls=%async_computation.7 | async-start | bytes 4194304
  335.7 2.5 copy-start.19
  346.3 1.0 copy-start.5
  347.3 11.3 %collective-permute-start.1 = (f32[128,768]{1,0:T(8,128)S(1)}, f32[128,768]{1,0:T(8,128)S(1)}, u32[]{:S(2)}, u32[]{:S(2)}) collective-permute-start(f32[128,768]{1,0:T(8,128)S(1)} %copy-done.5), channel_id=1, source_target_pairs={{0,8},{8,0},{16,24},{24,16},{1,9},{9,1},{17,25},{25,17},{2,10},{10... | collective-permute-start | bytes 1179656 | tf_op jit(solution)/shard_map/ppermute | solution.py:565
Sparse Core Ops, SparseCore 0:
  11.5 63.8 all-gather.4
  78.9 106.9 all-gather.6
  317.6 107.0 reduce-scatter.2
  431.6 161.9 reduce-scatter.4
